TPU v7x, 32 devices: a whole 2x2x4 slice. The times are simulated.
32 devices in a mesh: layer: 16 (over z, x, core), row: 2 (over y).
Axes of the slice: x: 2, y: 2, z: 4, core: 2. Of those that a mesh axis runs over, the one named last changes fastest.
Arguments:
- waves: bfloat16 [16, 3072, 512], P('layer', 'row'), may hold values from -6 to 6
- operators: bfloat16 [16, 4, 3072, 3072], P('layer', None, 'row'), may hold values from -0.0546875 to 0.0546875
- sources: bfloat16 [3072, 512], P('row'), may hold values from -6 to 6
- source_layer: int32 [128], replicated, may hold values from 0 to 15
Outputs:
- traces: bfloat16 [16, 3072, 512], P('layer', 'row')
All inputs are finite; a program needn't handle non-finite values.
Results may differ from a plain program's by a relative error of at most 0.0057.
Values may be sent and summed in bfloat16 or wider, within the bound.
A program may use at most 128 MiB of HBM per device.

v0:
```python
import jax
import jax.numpy as jnp
from jax import lax
from jax.sharding import PartitionSpec as P

TICKS = 3


def shifted(array, axis, by):
    peers = lax.axis_size(axis)
    pairs = [(i, i + by) for i in range(peers) if 0 <= i + by < peers]
    return lax.ppermute(array, axis, pairs)


def combine(real_prod, imag_prod, shot_count):
    real_part = real_prod[:, :shot_count] - imag_prod[:, shot_count:]
    imag_part = real_prod[:, shot_count:] + imag_prod[:, :shot_count]
    return jnp.concatenate([real_part, imag_part], axis=1)


def per_device(waves, operators, sources, source_layer):
    tile_rows = operators.shape[2]
    full_rows = operators.shape[3]
    column_count = waves.shape[2]
    shot_count = column_count // 4
    half = 2 * shot_count
    stacked = operators[0].reshape(4 * tile_rows, full_rows)
    layer_id = lax.axis_index("layer")
    shot_mask = jnp.tile((source_layer == layer_id).astype(jnp.float32), 4)
    source_term = sources.astype(jnp.float32) * shot_mask[None, :]
    current = waves[0]
    for sweep_tick in range(TICKS):
        products = jnp.dot(
            stacked,
            lax.all_gather(current, "row", axis=0, tiled=True),
            preferred_element_type=jnp.float32,
        )
        products = products.reshape(4, tile_rows, column_count)
        down_out = combine(products[0][:, :half], products[1][:, :half], shot_count) + combine(
            products[2][:, half:], products[3][:, half:], shot_count
        )
        up_out = combine(products[0][:, half:], products[1][:, half:], shot_count) + combine(
            products[2][:, :half], products[3][:, :half], shot_count
        )
        down_out = (down_out + source_term[:, :half]).astype(jnp.bfloat16)
        up_out = (up_out + source_term[:, half:]).astype(jnp.bfloat16)
        down_next = shifted(down_out, "layer", 1)
        up_next = shifted(up_out, "layer", -1)
        current = jnp.concatenate([down_next, up_next], axis=1)
    return current[None]


def solution(mesh):
    return jax.shard_map(
        per_device,
        mesh=mesh,
        in_specs=(P("layer", "row", None), P("layer", None, "row", None), P("row", None), P()),
        out_specs=P("layer", "row", None),
        check_vma=False,
    )
```

profile of v0, /device:TPU:9, one launch (start us, length us, event | category | flops | bytes accessed | tf_op | source)
XLA Modules:
  0.0 324.4 jit_solution(11651561303536006612)
XLA Ops:
  7.9 1.6 copy.5
  9.5 1.7 convert_multiply_fusion
  11.2 43.6 %all-gather.9.cloned.1.call-done = bf16[1,3072,512]{2,1,0:T(8,128)(2,1)} async-done(((bf16[1,1536,512]{2,1,0:T(8,128)(2,1)}), bf16[1,3072,512]{2,1,0:T(8,128)(2,1)}) %all-gather.9.cloned.1.call-update) | async-done | bytes 3145744 | tf_op jit(solution)/shard_map/all_gather | solution.py:35
  54.8 26.8 %fusion = f32[6144,512]{0,1:T(8,128)} fusion(bf16[6144,3072]{1,0:T(8,128)(2,1)} %bitcast.17, bf16[1,3072,512]{2,1,0:T(8,128)(2,1)} %all-gather.9.cloned.1.call-done), kind=kOutput, calls=%fused_computation.2 | convolution fusion | flops 19327352832 | bytes 53477376 | tf_op jit(solution)/shard_map/dot_general | solution.py:33
  81.6 6.0 %slice_subtract_fusion.10 = (f32[1536,128]{0,1:T(8,128)S(1)}, f32[1536,128]{0,1:T(8,128)S(1)}, f32[1536,128]{0,1:T(8,128)S(1)}, f32[1536,128]{0,1:T(8,128)S(1)},...) fusion(f32[6144,512]{0,1:T(8,128)} %fusion), kind=kLoop, calls=%fused_computation.47 | loop fusion | flops 1572864 | bytes 18874368 | tf_op jit(solution)/shard_map/sub | solution.py:16
  88.7 3.8 %collective-permute-start = (bf16[1536,256]{0,1:T(8,128)(2,1)S(1)}, bf16[1536,256]{0,1:T(8,128)(2,1)S(1)}, u32[]{:S(2)}, u32[]{:S(2)}) collective-permute-start(bf16[1536,256]{0,1:T(8,128)(2,1)S(1)} %get-tuple-element.33), channel_id=1, source_target_pairs={{0,2},{2,4},{4,6},{6,8},{8,10},{10,12},{12,14},{14,16},{16,18},{18... | collective-permute-start | bytes 2359304 | tf_op jit(solution)/shard_map/ppermute | solution.py:12
  92.5 1.9 collective-permute-start.1
  94.5 15.4 %collective-permute-done = bf16[1536,256]{0,1:T(8,128)(2,1)S(1)} collective-permute-done((bf16[1536,256]{0,1:T(8,128)(2,1)S(1)}, bf16[1536,256]{0,1:T(8,128)(2,1)S(1)}, u32[]{:S(2)}, u32[]{:S(2)}) %collective-permute-start) | collective-permute-done | bytes 786464 | tf_op jit(solution)/shard_map/ppermute | solution.py:12
  109.9 1.6 collective-permute-done.1
  113.0 43.2 %all-gather.5.cloned.1.call-done = bf16[3072,512]{0,1:T(8,128)(2,1)} async-done(((bf16[1536,512]{0,1:T(8,128)(2,1)}), bf16[3072,512]{0,1:T(8,128)(2,1)}) %all-gather.5.cloned.1.call-update) | async-done | bytes 3145744 | tf_op jit(solution)/shard_map/all_gather | solution.py:35
  156.3 27.7 %convolution_bitcast_fusion.1 = f32[6144,512]{0,1:T(8,128)} fusion(bf16[3072,512]{0,1:T(8,128)(2,1)} %all-gather.5.cloned.1.call-done, bf16[6144,3072]{1,0:T(8,128)(2,1)} %bitcast.18), kind=kOutput, calls=%fused_computation.1 | convolution fusion | flops 19327352832 | bytes 53477376 | tf_op jit(solution)/shard_map/dot_general | solution.py:33
  184.0 6.0 %slice_subtract_fusion.6 = (f32[1536,128]{0,1:T(8,128)S(1)}, f32[1536,128]{0,1:T(8,128)S(1)}, f32[1536,128]{0,1:T(8,128)S(1)}, f32[1536,128]{0,1:T(8,128)S(1)}, ...) fusion(f32[6144,512]{0,1:T(8,128)} %convolution_bitcast_fusion.1), kind=kLoop, calls=%fused_computation.39 | loop fusion | flops 1572864 | bytes 18874368 | tf_op jit(solution)/shard_map/sub | solution.py:16
  191.1 3.8 %collective-permute-start.2 = (bf16[1536,256]{0,1:T(8,128)(2,1)S(1)}, bf16[1536,256]{0,1:T(8,128)(2,1)S(1)}, u32[]{:S(2)}, u32[]{:S(2)}) collective-permute-start(bf16[1536,256]{0,1:T(8,128)(2,1)S(1)} %get-tuple-element.31), channel_id=1, source_target_pairs={{0,2},{2,4},{4,6},{6,8},{8,10},{10,12},{12,14},{14,16},{16,18},{18... | collective-permute-start | bytes 2359304 | tf_op jit(solution)/shard_map/ppermute | solution.py:12
  194.9 2.1 collective-permute-start.3
  197.1 15.2 %collective-permute-done.2 = bf16[1536,256]{0,1:T(8,128)(2,1)S(1)} collective-permute-done((bf16[1536,256]{0,1:T(8,128)(2,1)S(1)}, bf16[1536,256]{0,1:T(8,128)(2,1)S(1)}, u32[]{:S(2)}, u32[]{:S(2)}) %collective-permute-start.2) | collective-permute-done | bytes 786464 | tf_op jit(solution)/shard_map/ppermute | solution.py:12
  212.3 1.6 collective-permute-done.3
  215.1 43.5 %all-gather.7.cloned.1.call-done = bf16[3072,512]{0,1:T(8,128)(2,1)} async-done(((bf16[1536,512]{0,1:T(8,128)(2,1)}), bf16[3072,512]{0,1:T(8,128)(2,1)}) %all-gather.7.cloned.1.call-update) | async-done | bytes 3145744 | tf_op jit(solution)/shard_map/all_gather | solution.py:35
  258.6 27.7 %convolution_bitcast_fusion = f32[6144,512]{0,1:T(8,128)} fusion(bf16[3072,512]{0,1:T(8,128)(2,1)} %all-gather.7.cloned.1.call-done, bf16[6144,3072]{1,0:T(8,128)(2,1)} %bitcast.19), kind=kOutput, calls=%fused_computation | convolution fusion | flops 19327352832 | bytes 53477376 | tf_op jit(solution)/shard_map/dot_general | solution.py:33
  286.3 6.0 %slice_subtract_fusion.2 = (f32[1536,128]{0,1:T(8,128)S(1)}, f32[1536,128]{0,1:T(8,128)S(1)}, f32[1536,128]{0,1:T(8,128)S(1)}, f32[1536,128]{0,1:T(8,128)S(1)}, ...) fusion(f32[6144,512]{0,1:T(8,128)} %convolution_bitcast_fusion), kind=kLoop, calls=%fused_computation.31 | loop fusion | flops 1572864 | bytes 18874368 | tf_op jit(solution)/shard_map/sub | solution.py:16
  293.4 3.8 %collective-permute-start.4 = (bf16[1536,256]{0,1:T(8,128)(2,1)S(1)}, bf16[1536,256]{0,1:T(8,128)(2,1)S(1)}, u32[]{:S(2)}, u32[]{:S(2)}) collective-permute-start(bf16[1536,256]{0,1:T(8,128)(2,1)S(1)} %get-tuple-element.29), channel_id=1, source_target_pairs={{0,2},{2,4},{4,6},{6,8},{8,10},{10,12},{12,14},{14,16},{16,18},{18... | collective-permute-start | bytes 2359304 | tf_op jit(solution)/shard_map/ppermute | solution.py:12
  297.3 1.9 collective-permute-start.5
  299.2 15.4 %collective-permute-done.4 = bf16[1536,256]{0,1:T(8,128)(2,1)S(1)} collective-permute-done((bf16[1536,256]{0,1:T(8,128)(2,1)S(1)}, bf16[1536,256]{0,1:T(8,128)(2,1)S(1)}, u32[]{:S(2)}, u32[]{:S(2)}) %collective-permute-start.4) | collective-permute-done | bytes 786464 | tf_op jit(solution)/shard_map/ppermute | solution.py:12
  314.6 1.6 collective-permute-done.5
  316.3 1.6 copy.6
  (18 shorter events, 7.6 us)
Async XLA Ops:
  6.5 1.4 copy-start
  6.5 48.3 %all-gather.9.cloned.1.call-start = ((), (), s32[]{:S(2)}) async-start(), calls=%async_computation.2 | async-start | bytes 4718592 | tf_op jit(solution)/shard_map/all_gather | solution.py:35
  7.3 149.0 %all-gather.5.cloned.1.call-start = ((), (), s32[]{:S(2)}) async-start(), calls=%async_computation | async-start | bytes 4718592 | tf_op jit(solution)/shard_map/all_gather | solution.py:35
  7.9 1.6 copy-start.1
  88.7 21.2 %collective-permute-start = (bf16[1536,256]{0,1:T(8,128)(2,1)S(1)}, bf16[1536,256]{0,1:T(8,128)(2,1)S(1)}, u32[]{:S(2)}, u32[]{:S(2)}) collective-permute-start(bf16[1536,256]{0,1:T(8,128)(2,1)S(1)} %get-tuple-element.33), channel_id=1, source_target_pairs={{0,2},{2,4},{4,6},{6,8},{8,10},{10,12},{12,14},{14,16},{16,18},{18... | collective-permute-start | bytes 2359304 | tf_op jit(solution)/shard_map/ppermute | solution.py:12
  92.5 19.0 %collective-permute-start.1 = (bf16[1536,256]{0,1:T(8,128)(2,1)S(1)}, bf16[1536,256]{0,1:T(8,128)(2,1)S(1)}, u32[]{:S(2)}, u32[]{:S(2)}) collective-permute-start(bf16[1536,256]{0,1:T(8,128)(2,1)S(1)} %get-tuple-element.34), channel_id=1, source_target_pairs={{2,0},{4,2},{6,4},{8,6},{10,8},{12,10},{14,12},{16,14},{18,16},{20... | collective-permute-start | bytes 2359304 | tf_op jit(solution)/shard_map/ppermute | solution.py:12
  112.8 145.8 %all-gather.7.cloned.1.call-start = ((), (), s32[]{:S(2)}) async-start(), calls=%async_computation.1 | async-start | bytes 4718592 | tf_op jit(solution)/shard_map/all_gather | solution.py:35
  191.1 21.2 %collective-permute-start.2 = (bf16[1536,256]{0,1:T(8,128)(2,1)S(1)}, bf16[1536,256]{0,1:T(8,128)(2,1)S(1)}, u32[]{:S(2)}, u32[]{:S(2)}) collective-permute-start(bf16[1536,256]{0,1:T(8,128)(2,1)S(1)} %get-tuple-element.31), channel_id=1, source_target_pairs={{0,2},{2,4},{4,6},{6,8},{8,10},{10,12},{12,14},{14,16},{16,18},{18... | collective-permute-start | bytes 2359304 | tf_op jit(solution)/shard_map/ppermute | solution.py:12
  194.9 19.0 %collective-permute-start.3 = (bf16[1536,256]{0,1:T(8,128)(2,1)S(1)}, bf16[1536,256]{0,1:T(8,128)(2,1)S(1)}, u32[]{:S(2)}, u32[]{:S(2)}) collective-permute-start(bf16[1536,256]{0,1:T(8,128)(2,1)S(1)} %get-tuple-element.32), channel_id=1, source_target_pairs={{2,0},{4,2},{6,4},{8,6},{10,8},{12,10},{14,12},{16,14},{18,16},{20... | collective-permute-start | bytes 2359304 | tf_op jit(solution)/shard_map/ppermute | solution.py:12
  293.4 21.2 %collective-permute-start.4 = (bf16[1536,256]{0,1:T(8,128)(2,1)S(1)}, bf16[1536,256]{0,1:T(8,128)(2,1)S(1)}, u32[]{:S(2)}, u32[]{:S(2)}) collective-permute-start(bf16[1536,256]{0,1:T(8,128)(2,1)S(1)} %get-tuple-element.29), channel_id=1, source_target_pairs={{0,2},{2,4},{4,6},{6,8},{8,10},{10,12},{12,14},{14,16},{16,18},{18... | collective-permute-start | bytes 2359304 | tf_op jit(solution)/shard_map/ppermute | solution.py:12
  297.3 19.0 %collective-permute-start.5 = (bf16[1536,256]{0,1:T(8,128)(2,1)S(1)}, bf16[1536,256]{0,1:T(8,128)(2,1)S(1)}, u32[]{:S(2)}, u32[]{:S(2)}) collective-permute-start(bf16[1536,256]{0,1:T(8,128)(2,1)S(1)} %get-tuple-element.30), channel_id=1, source_target_pairs={{2,0},{4,2},{6,4},{8,6},{10,8},{12,10},{14,12},{16,14},{18,16},{20... | collective-permute-start | bytes 2359304 | tf_op jit(solution)/shard_map/ppermute | solution.py:12
Sparse Core Ops, SparseCore 0:
  8.9 45.8 all-gather.8
  112.9 43.3 all-gather.4
  215.3 43.3 all-gather.6
where the time goes:
time: 325 us; the launch traced here: 324 us
  waiting for transfers between devices  182 us (56%)
  matrix products  82.2 us (25%)
  other arithmetic  25.6 us (8%)
  starting transfers between devices  17.7 us (5%)
  between operations  13.2 us (4%)
  local copies, waits for them, and re-layouts  3.78 us (1%)
    all_gather x3, waiting for transfers between devices, per_device(): lax.all_gather(current, 'row', axis=0, tiled=True)  130 us
    dot_general x3, matrix products, per_device(): jnp.dot(stacked, lax.all_gather(current, 'row', axis=0, tiled=True), pref...  82.2 us
    ppermute x6, waiting for transfers between devices, shifted(): return lax.ppermute(array, axis, pairs)  50.9 us
    sub x3, other arithmetic, combine(): real_part = real_prod[:, :shot_count] - imag_prod[:, shot_count:]  17.9 us
    ppermute x6, starting transfers between devices, shifted(): return lax.ppermute(array, axis, pairs)  17.4 us
  transfers between devices with their start and end apart: 9, of which 9 were waited for; matrix products, arithmetic and copies ran while one was open for 1% of the time, Pallas kernels for 0%

commit v1 on v0

v1 whole, which is shorter than its diff:
```python
import functools
import math

import jax
import jax.numpy as jnp
from jax import lax
from jax.experimental import pallas as pl
from jax.experimental.pallas import tpu as pltpu
from jax.sharding import PartitionSpec as P

TICKS = 3
MESH = pl.DeviceIdType.MESH


def swap_halves(first, second):
    half = first.shape[1] // 2
    low = lax.broadcasted_iota(jnp.int32, first.shape, 1) < half
    return (
        jnp.where(low, first, pltpu.roll(second, half, 1)),
        jnp.where(low, pltpu.roll(first, half, 1), second),
    )


def kernel(
    layers, row_parts, chunk,
    waves, operators, sources, source_layer, traces,
    held, current, turned, outgoing, final, source_term,
    load_sem, first_send, send_sem, recv_sem, final_sem,
):
    layer = lax.axis_index("layer")
    part = lax.axis_index("row")
    rows, lanes = outgoing.shape[3], outgoing.shape[4]
    depth = current.shape[3]
    chunks = rows // chunk
    has_above, has_below = layer > 0, layer < layers - 1

    def load(i):
        span = pl.ds(pl.multiple_of(i * chunk, chunk), chunk)
        return pltpu.make_async_copy(operators.at[0, :, span, :], held.at[:, span, :], load_sem.at[i])

    barrier = pltpu.get_barrier_semaphore()
    for d in range(1, row_parts):
        pl.semaphore_signal(barrier, inc=1, device_id=(layer, lax.rem(part + d, row_parts)), device_id_type=MESH)
    for present, other in ((has_above, layer - 1), (has_below, layer + 1)):
        @pl.when(present)
        def _():
            for p in range(row_parts):
                pl.semaphore_signal(barrier, inc=1, device_id=(other, p), device_id_type=MESH)

    def pack(source_of, put):
        @pl.loop(0, chunks)
        def _(i):
            span = pl.ds(pl.multiple_of(i * chunk, chunk), chunk)
            for way in range(2):
                re = source_of(span, 2 * way)
                im = source_of(span, 2 * way + 1)
                for group, packed in enumerate(swap_halves(re, im)):
                    put(i, group, way, packed.astype(jnp.bfloat16))

    def put_wave(i, group, way, packed):
        current[0, group, way, pl.ds(pl.multiple_of(part * rows + i * chunk, chunk), chunk), :] = packed

    pack(lambda span, q: waves[0, span, q * lanes:(q + 1) * lanes].astype(jnp.float32), put_wave)

    peers = row_parts - 1 + row_parts * (has_above.astype(jnp.int32) + has_below.astype(jnp.int32))
    pl.semaphore_wait(barrier, peers)

    own = pl.ds(pl.multiple_of(part * rows, chunk), rows)
    for group in range(2):
        for way in range(2):
            for d in range(1, row_parts):
                pltpu.make_async_remote_copy(
                    src_ref=current.at[0, group, way, own, :],
                    dst_ref=current.at[0, group, way, own, :],
                    send_sem=first_send.at[group, way, d - 1],
                    recv_sem=recv_sem.at[0, group, way, part],
                    device_id=(layer, lax.rem(part + d, row_parts)),
                    device_id_type=MESH,
                ).start()

    for i in range(chunks):
        load(i).start()

    mask = (source_layer[...] == layer).astype(jnp.float32)

    def put_source(i, group, way, packed):
        source_term[group, way, pl.ds(pl.multiple_of(i * chunk, chunk), chunk), :] = packed

    pack(lambda span, q: sources[span, q * lanes:(q + 1) * lanes].astype(jnp.float32) * mask, put_source)

    for way, present in ((0, has_above), (1, has_below)):
        @pl.when(jnp.logical_not(present))
        def _():
            for group in range(2):
                final[group, way] = jnp.zeros((rows, lanes), jnp.bfloat16)
                for tick in range(1, TICKS):
                    @pl.loop(0, depth // chunk)
                    def _(i):
                        span = pl.ds(pl.multiple_of(i * chunk, chunk), chunk)
                        current[tick, group, way, span, :] = jnp.zeros((chunk, lanes), jnp.bfloat16)

    def arrived(tick, group, way, p):
        ref = current.at[tick, group, way, pl.ds(p * rows, rows), :]
        pltpu.make_async_copy(ref, ref, recv_sem.at[tick, group, way, p]).wait()

    @pl.loop(0, 2 * TICKS)
    def _(step):
        tick, group = step // 2, step % 2

        @pl.when(tick == 0)
        def _():
            for p in range(row_parts):
                @pl.when(p != part)
                def _():
                    arrived(tick, group, 0, p)
                    arrived(tick, group, 1, p)

        for way, present in ((0, has_above), (1, has_below)):
            @pl.when(jnp.logical_and(tick > 0, present))
            def _():
                for p in range(row_parts):
                    arrived(tick, group, way, p)

        @pl.loop(0, depth // chunk)
        def _(i):
            span = pl.ds(pl.multiple_of(i * chunk, chunk), chunk)
            low = lax.broadcasted_iota(jnp.int32, (chunk, lanes), 1) < lanes // 2
            for way in range(2):
                rolled = pltpu.roll(current[tick, group, way, span, :].astype(jnp.float32), lanes // 2, 1)
                turned[way, span, :] = jnp.where(low, -rolled, rolled).astype(jnp.bfloat16)

        @pl.loop(0, chunks)
        def _(i):
            span = pl.ds(pl.multiple_of(i * chunk, chunk), chunk)

            @pl.when(step == 0)
            def _():
                load(i).wait()

            down, up = current[tick, group, 0], current[tick, group, 1]
            down_turned, up_turned = turned[0], turned[1]
            total = jnp.dot(held[0, span, :], jnp.concatenate([down, up], 1), preferred_element_type=jnp.float32)
            total += jnp.dot(held[1, span, :], jnp.concatenate([down_turned, up_turned], 1), preferred_element_type=jnp.float32)
            total += jnp.dot(held[2, span, :], jnp.concatenate([up, down], 1), preferred_element_type=jnp.float32)
            total += jnp.dot(held[3, span, :], jnp.concatenate([up_turned, down_turned], 1), preferred_element_type=jnp.float32)
            for way in range(2):
                value = total[:, way * lanes:(way + 1) * lanes] + source_term[group, way, span, :].astype(jnp.float32)
                outgoing[tick, group, way, span, :] = value.astype(jnp.bfloat16)

            there = pl.ds(pl.multiple_of(part * rows + i * chunk, chunk), chunk)
            for way, present, other in ((0, has_below, layer + 1), (1, has_above, layer - 1)):
                @pl.when(jnp.logical_and(present, tick < TICKS - 1))
                def _():
                    for d in range(row_parts - 1, -1, -1):
                        pltpu.make_async_remote_copy(
                            src_ref=outgoing.at[tick, group, way, span, :],
                            dst_ref=current.at[tick + 1, group, way, there, :],
                            send_sem=send_sem.at[tick, group, way, d],
                            recv_sem=recv_sem.at[tick + 1, group, way, part],
                            device_id=(other, lax.rem(part + d, row_parts)),
                            device_id_type=MESH,
                        ).start()

                @pl.when(jnp.logical_and(present, tick == TICKS - 1))
                def _():
                    pltpu.make_async_remote_copy(
                        src_ref=outgoing.at[tick, group, way, span, :],
                        dst_ref=final.at[group, way, span, :],
                        send_sem=send_sem.at[tick, group, way, 0],
                        recv_sem=final_sem.at[group, way],
                        device_id=(other, part),
                        device_id_type=MESH,
                    ).start()

    for way, present in ((0, has_above), (1, has_below)):
        @pl.when(present)
        def _():
            for group in range(2):
                ref = final.at[group, way]
                pltpu.make_async_copy(ref, ref, final_sem.at[group, way]).wait()

    @pl.loop(0, chunks)
    def _(i):
        span = pl.ds(pl.multiple_of(i * chunk, chunk), chunk)
        for way in range(2):
            a = final[0, way, span, :].astype(jnp.float32)
            b = final[1, way, span, :].astype(jnp.float32)
            for q, block in enumerate(swap_halves(a, b)):
                at = (2 * way + q) * lanes
                traces[0, span, at:at + lanes] = block.astype(jnp.bfloat16)

    for group in range(2):
        for way, present in ((0, has_below), (1, has_above)):
            for d in range(1, row_parts):
                ref = current.at[0, group, way, own, :]
                pltpu.make_async_copy(ref, ref, first_send.at[group, way, d - 1]).wait()

            @pl.when(present)
            def _():
                for tick in range(TICKS):
                    for d in range(row_parts if tick < TICKS - 1 else 1):
                        ref = outgoing.at[tick, group, way]
                        pltpu.make_async_copy(ref, ref, send_sem.at[tick, group, way, d]).wait()


def per_device(waves, operators, sources, source_layer):
    layers, row_parts = lax.axis_size("layer"), lax.axis_size("row")
    rows, depth = operators.shape[2], operators.shape[3]
    lanes = waves.shape[2] // 4
    chunk = math.gcd(rows, 256)
    vmem = pl.BlockSpec(memory_space=pltpu.VMEM)
    return pl.pallas_call(
        functools.partial(kernel, layers, row_parts, chunk),
        out_shape=jax.ShapeDtypeStruct(waves.shape, jnp.bfloat16),
        in_specs=[vmem, pl.BlockSpec(memory_space=pl.ANY), vmem, vmem],
        out_specs=vmem,
        scratch_shapes=[
            pltpu.VMEM((4, rows, depth), jnp.bfloat16),
            pltpu.VMEM((TICKS, 2, 2, depth, lanes), jnp.bfloat16),
            pltpu.VMEM((2, depth, lanes), jnp.bfloat16),
            pltpu.VMEM((TICKS, 2, 2, rows, lanes), jnp.bfloat16),
            pltpu.VMEM((2, 2, rows, lanes), jnp.bfloat16),
            pltpu.VMEM((2, 2, rows, lanes), jnp.bfloat16),
            pltpu.SemaphoreType.DMA((rows // chunk,)),
            pltpu.SemaphoreType.DMA((2, 2, max(row_parts - 1, 1))),
            pltpu.SemaphoreType.DMA((TICKS, 2, 2, row_parts)),
            pltpu.SemaphoreType.DMA((TICKS, 2, 2, row_parts)),
            pltpu.SemaphoreType.DMA((2, 2)),
        ],
        compiler_params=pltpu.CompilerParams(
            collective_id=0, has_side_effects=True, vmem_limit_bytes=67043328
        ),
    )(waves, operators, sources, source_layer.reshape(1, lanes))


def solution(mesh):
    return jax.shard_map(
        per_device,
        mesh=mesh,
        in_specs=(P("layer", "row", None), P("layer", None, "row", None), P("row", None), P()),
        out_specs=P("layer", "row", None),
        check_vma=False,
    )
```

time: 325 us -> 131 us (0.40)
  waiting for transfers between devices: 182 us -> 0 us
  Pallas kernels: 0 us -> 126 us
  matrix products: 82.2 us -> 0 us
  other arithmetic: 25.6 us -> 0 us
  starting transfers between devices: 17.7 us -> 0 us
  between operations: 13.2 us -> 0.01 us
    all_gather x3 -> x0, waiting for transfers between devices: 130 us -> none  [per_device(): lax.all_gather(current, 'row', axis=0, tiled=True)]
    pallas_call x0 -> x1, Pallas kernels: none -> 126 us  [per_device(): pl.pallas_call(functools.partial(kernel, layers, row_parts, chunk), out_s...]
    dot_general x3 -> x0, matrix products: 82.2 us -> none  [per_device(): jnp.dot(stacked, lax.all_gather(current, 'row', axis=0, tiled=True), pref...]
    ppermute x6 -> x0, waiting for transfers between devices: 50.9 us -> none  [shifted(): return lax.ppermute(array, axis, pairs)]
    sub x3 -> x0, other arithmetic: 17.9 us -> none  [combine(): real_part = real_prod[:, :shot_count] - imag_prod[:, shot_count:]]
    ppermute x6 -> x0, starting transfers between devices: 17.4 us -> none  [shifted(): return lax.ppermute(array, axis, pairs)]
    convert_element_type x4 -> x0, other arithmetic: 3.4 us -> none  [the longest x3 3.4 us: per_device(): down_out = (down_out + source_term[:, :half]).astype(jnp.bfloat16)]
  transfers between devices with their start and end apart: 9 -> 0, of which waited for: 9 -> 0; matrix products, arithmetic and copies ran while one was open for 1% -> 0% of each run, Pallas kernels for 0% -> 0%
where the time goes in v1:
time: 131 us; the launch traced here: 129 us
  Pallas kernels  126 us (96%)
  local copies, waits for them, and re-layouts  2.65 us (2%)
    pallas_call x1, Pallas kernels, per_device(): pl.pallas_call(functools.partial(kernel, layers, row_parts, chunk), out_s...  126 us
    unnamed x1, local copies, waits for them, and re-layouts  2.65 us

profile of v1, /device:TPU:9, one launch (start us, length us, event | category | flops | bytes accessed | tf_op | source)
XLA Modules:
  0.0 129.0 jit_solution(809534783752879776)
XLA Ops:
  0.0 126.4 %shard_map.46 = bf16[1,1536,512]{2,1,0:T(8,128)(2,1)} custom-call(bf16[1,1536,512]{2,1,0:T(8,128)(2,1)} %waves.1, bf16[1,4,1536,3072]{3,2,1,0:T(8,128)(2,1)} %operators.1, bf16[1536,512]{1,0:T(8,128)(2,1)} %sources.1, s32[1,128]{1,0:T(1,128)} %bitcast.1), custom_call_target="tpu_custom_call" | custom-call | tf_op jit(solution)/shard_map/pallas_call | solution.py:212
  126.4 2.7 %copy.6 = bf16[1,1536,512]{2,1,0:T(8,128)(2,1)} copy(bf16[1,1536,512]{2,1,0:T(8,128)(2,1)} %shard_map.46) | data formatting | bytes 3145728

commit v2 on v1

v2 whole, which is shorter than its diff:
```python
import functools
import math

import jax
import jax.numpy as jnp
from jax import lax
from jax.experimental import pallas as pl
from jax.experimental.pallas import tpu as pltpu
from jax.sharding import PartitionSpec as P

TICKS = 3
MESH = pl.DeviceIdType.MESH


def swap_halves(first, second):
    half = first.shape[1] // 2
    low = lax.broadcasted_iota(jnp.int32, first.shape, 1) < half
    return (
        jnp.where(low, first, pltpu.roll(second, half, 1)),
        jnp.where(low, pltpu.roll(first, half, 1), second),
    )


def kernel(
    layers, row_parts, chunk, big,
    waves, operators, sources, source_layer, traces,
    held, current, turned, total, outgoing, final, source_term, stage,
    stage_sem, load_sem, store_sem, first_send, send_sem, recv_sem, final_sem,
):
    layer = lax.axis_index("layer")
    part = lax.axis_index("row")
    rows, lanes = outgoing.shape[3], outgoing.shape[4]
    depth = current.shape[3]
    chunks = rows // chunk
    has_above, has_below = layer > 0, layer < layers - 1

    def piece(i, size=chunk, base=0):
        return pl.ds(pl.multiple_of(base + i * size, chunk), size)

    def load(i):
        span = piece(i, big)
        return pltpu.make_async_copy(operators.at[0, :, span, :], held.at[:, span, :], load_sem.at[i])

    wave_load = pltpu.make_async_copy(waves.at[0], stage, stage_sem.at[0])
    source_load = pltpu.make_async_copy(sources, stage, stage_sem.at[1])
    wave_load.start()

    barrier = pltpu.get_barrier_semaphore()
    for d in range(1, row_parts):
        pl.semaphore_signal(barrier, inc=1, device_id=(layer, lax.rem(part + d, row_parts)), device_id_type=MESH)
    for present, other in ((has_above, layer - 1), (has_below, layer + 1)):
        @pl.when(present)
        def _():
            for p in range(row_parts):
                pl.semaphore_signal(barrier, inc=1, device_id=(other, p), device_id_type=MESH)

    wave_load.wait()
    for i in range(rows // big):
        load(i).start()

    def packed(span):
        for way in range(2):
            at = 2 * way * lanes
            re = stage[span, at:at + lanes].astype(jnp.float32)
            im = stage[span, at + lanes:at + 2 * lanes].astype(jnp.float32)
            yield way, swap_halves(re, im)

    own_base = part * rows

    @pl.loop(0, chunks)
    def _(i):
        for way, groups in packed(piece(i)):
            for group in range(2):
                current[0, group, way, piece(i, chunk, own_base), :] = groups[group].astype(jnp.bfloat16)

    peers = row_parts - 1 + row_parts * (has_above.astype(jnp.int32) + has_below.astype(jnp.int32))
    pl.semaphore_wait(barrier, peers)

    own = piece(0, rows, own_base)
    for group in range(2):
        for way in range(2):
            for d in range(1, row_parts):
                pltpu.make_async_remote_copy(
                    src_ref=current.at[0, group, way, own, :],
                    dst_ref=current.at[0, group, way, own, :],
                    send_sem=first_send.at[group, way, d - 1],
                    recv_sem=recv_sem.at[0, group, way, part],
                    device_id=(layer, lax.rem(part + d, row_parts)),
                    device_id_type=MESH,
                ).start()

    source_load.start()
    source_load.wait()
    mask = (source_layer[...] == layer).astype(jnp.float32)
    pair = jnp.concatenate([mask, mask], 1)
    packed_mask = swap_halves(pair[:, :lanes], pair[:, lanes:])

    @pl.loop(0, chunks)
    def _(i):
        for way, groups in packed(piece(i)):
            for group in range(2):
                source_term[group, way, piece(i), :] = (groups[group] * packed_mask[group]).astype(jnp.bfloat16)

    for way, present in ((0, has_above), (1, has_below)):
        @pl.when(jnp.logical_not(present))
        def _():
            for group in range(2):
                final[group, way] = jnp.zeros((rows, lanes), jnp.bfloat16)
                for tick in range(1, TICKS):
                    @pl.loop(0, depth // chunk)
                    def _(i):
                        current[tick, group, way, piece(i), :] = jnp.zeros((chunk, lanes), jnp.bfloat16)

    def arrived(tick, group, way, p):
        ref = current.at[tick, group, way, piece(0, rows, p * rows), :]
        pltpu.make_async_copy(ref, ref, recv_sem.at[tick, group, way, p]).wait()

    def product(tick, group, span, inner):
        down, up = current[tick, group, 0, inner, :], current[tick, group, 1, inner, :]
        down_turned, up_turned = turned[0], turned[1]
        out = jnp.dot(held[0, span, inner], jnp.concatenate([down, up], 1), preferred_element_type=jnp.float32)
        out += jnp.dot(held[1, span, inner], jnp.concatenate([down_turned, up_turned], 1), preferred_element_type=jnp.float32)
        out += jnp.dot(held[2, span, inner], jnp.concatenate([up, down], 1), preferred_element_type=jnp.float32)
        out += jnp.dot(held[3, span, inner], jnp.concatenate([up_turned, down_turned], 1), preferred_element_type=jnp.float32)
        return out

    @pl.loop(0, 2 * TICKS)
    def _(step):
        tick, group = step // 2, step % 2
        for d in range(row_parts):
            p = lax.rem(part + d, row_parts)
            inner = pl.ds(pl.multiple_of(p * rows, 128), rows)
            if d > 0:
                @pl.when(tick == 0)
                def _():
                    arrived(tick, group, 0, p)
                    arrived(tick, group, 1, p)

            for way, present in ((0, has_above), (1, has_below)):
                @pl.when(jnp.logical_and(tick > 0, present))
                def _():
                    arrived(tick, group, way, p)

            @pl.loop(0, chunks)
            def _(i):
                low = lax.broadcasted_iota(jnp.int32, (chunk, lanes), 1) < lanes // 2
                for way in range(2):
                    block = current[tick, group, way, piece(i, chunk, p * rows), :]
                    rolled = pltpu.roll(block.astype(jnp.float32), lanes // 2, 1)
                    turned[way, piece(i), :] = jnp.where(low, -rolled, rolled).astype(jnp.bfloat16)

            if d < row_parts - 1:
                @pl.loop(0, rows // big)
                def _(i):
                    span = piece(i, big)
                    if d == 0:
                        @pl.when(step == 0)
                        def _():
                            load(i).wait()
                        total[span, :] = product(tick, group, span, inner)
                    else:
                        total[span, :] += product(tick, group, span, inner)
                continue

            @pl.loop(0, chunks)
            def _(i):
                span = piece(i)
                if row_parts == 1:
                    @pl.when(jnp.logical_and(step == 0, i % (big // chunk) == 0))
                    def _():
                        load(i // (big // chunk)).wait()
                out = product(tick, group, span, inner)
                if row_parts > 1:
                    out += total[span, :]
                for way in range(2):
                    value = out[:, way * lanes:(way + 1) * lanes] + source_term[group, way, span, :].astype(jnp.float32)
                    outgoing[tick, group, way, span, :] = value.astype(jnp.bfloat16)

                there = piece(i, chunk, own_base)
                for way, present, other in ((0, has_below, layer + 1), (1, has_above, layer - 1)):
                    @pl.when(jnp.logical_and(present, tick < TICKS - 1))
                    def _():
                        for e in range(row_parts - 1, -1, -1):
                            pltpu.make_async_remote_copy(
                                src_ref=outgoing.at[tick, group, way, span, :],
                                dst_ref=current.at[tick + 1, group, way, there, :],
                                send_sem=send_sem.at[tick, group, way, e],
                                recv_sem=recv_sem.at[tick + 1, group, way, part],
                                device_id=(other, lax.rem(part + e, row_parts)),
                                device_id_type=MESH,
                            ).start()

                    @pl.when(jnp.logical_and(present, tick == TICKS - 1))
                    def _():
                        pltpu.make_async_remote_copy(
                            src_ref=outgoing.at[tick, group, way, span, :],
                            dst_ref=final.at[group, way, span, :],
                            send_sem=send_sem.at[tick, group, way, 0],
                            recv_sem=final_sem.at[group, way, i],
                            device_id=(other, part),
                            device_id_type=MESH,
                        ).start()

    def store(i):
        return pltpu.make_async_copy(stage.at[piece(i), :], traces.at[0, piece(i), :], store_sem.at[i])

    @pl.loop(0, chunks)
    def _(i):
        span = piece(i)
        for way, present in ((0, has_above), (1, has_below)):
            @pl.when(present)
            def _():
                for group in range(2):
                    ref = final.at[group, way, span, :]
                    pltpu.make_async_copy(ref, ref, final_sem.at[group, way, i]).wait()
            a = final[0, way, span, :].astype(jnp.float32)
            b = final[1, way, span, :].astype(jnp.float32)
            for q, block in enumerate(swap_halves(a, b)):
                at = (2 * way + q) * lanes
                stage[span, at:at + lanes] = block.astype(jnp.bfloat16)
        store(i).start()

    for group in range(2):
        for way, present in ((0, has_below), (1, has_above)):
            for d in range(1, row_parts):
                ref = current.at[0, group, way, own, :]
                pltpu.make_async_copy(ref, ref, first_send.at[group, way, d - 1]).wait()

            @pl.when(present)
            def _():
                for tick in range(TICKS):
                    for d in range(row_parts if tick < TICKS - 1 else 1):
                        ref = outgoing.at[tick, group, way]
                        pltpu.make_async_copy(ref, ref, send_sem.at[tick, group, way, d]).wait()

    for i in range(chunks):
        store(i).wait()


def per_device(waves, operators, sources, source_layer):
    layers, row_parts = lax.axis_size("layer"), lax.axis_size("row")
    rows, depth = operators.shape[2], operators.shape[3]
    lanes = waves.shape[2] // 4
    chunk, big = math.gcd(rows, 256), math.gcd(rows, 512)
    anywhere = pl.BlockSpec(memory_space=pl.ANY)
    traces = pl.pallas_call(
        functools.partial(kernel, layers, row_parts, chunk, big),
        out_shape=jax.ShapeDtypeStruct(waves.shape, jnp.bfloat16),
        in_specs=[anywhere, anywhere, anywhere, pl.BlockSpec(memory_space=pltpu.VMEM)],
        out_specs=anywhere,
        scratch_shapes=[
            pltpu.VMEM((4, rows, depth), jnp.bfloat16),
            pltpu.VMEM((TICKS, 2, 2, depth, lanes), jnp.bfloat16),
            pltpu.VMEM((2, rows, lanes), jnp.bfloat16),
            pltpu.VMEM((rows, 2 * lanes), jnp.float32),
            pltpu.VMEM((TICKS, 2, 2, rows, lanes), jnp.bfloat16),
            pltpu.VMEM((2, 2, rows, lanes), jnp.bfloat16),
            pltpu.VMEM((2, 2, rows, lanes), jnp.bfloat16),
            pltpu.VMEM((rows, 4 * lanes), jnp.bfloat16),
            pltpu.SemaphoreType.DMA((2,)),
            pltpu.SemaphoreType.DMA((rows // big,)),
            pltpu.SemaphoreType.DMA((rows // chunk,)),
            pltpu.SemaphoreType.DMA((2, 2, max(row_parts - 1, 1))),
            pltpu.SemaphoreType.DMA((TICKS, 2, 2, row_parts)),
            pltpu.SemaphoreType.DMA((TICKS, 2, 2, row_parts)),
            pltpu.SemaphoreType.DMA((2, 2, rows // chunk)),
        ],
        compiler_params=pltpu.CompilerParams(
            collective_id=0, has_side_effects=True, vmem_limit_bytes=67043328
        ),
    )(waves, operators, sources, source_layer.reshape(1, lanes))
    layer = lax.axis_index("layer")
    upgoing = lax.broadcasted_iota(jnp.int32, waves.shape, 2) >= 2 * lanes
    edge = jnp.where(upgoing, layer == layers - 1, layer == 0)
    return jnp.where(edge, jnp.zeros_like(traces), traces)


def solution(mesh):
    return jax.shard_map(
        per_device,
        mesh=mesh,
        in_specs=(P("layer", "row", None), P("layer", None, "row", None), P("row", None), P()),
        out_specs=P("layer", "row", None),
        check_vma=False,
    )
```

time: 131 us -> 129 us (0.985); the launches traced: 129 us -> 129 us
  other arithmetic: 0 us -> 3.2 us
  local copies, waits for them, and re-layouts: 2.65 us -> 0 us
    select_n x0 -> x2, other arithmetic: none -> 3.2 us  [the longest x1 2.66 us: per_device(): return jnp.where(edge, jnp.zeros_like(traces), traces)]
    unnamed x1 -> x0, local copies, waits for them, and re-layouts: 2.65 us -> none
where the time goes in v2:
time: 129 us
  Pallas kernels  125 us (97%)
  other arithmetic  3.2 us (2%)
    pallas_call x1, Pallas kernels, per_device(): pl.pallas_call(functools.partial(kernel, layers, row_parts, chunk, big),...  125 us
    select_n x1, other arithmetic, per_device(): return jnp.where(edge, jnp.zeros_like(traces), traces)  2.66 us

profile of v2, /device:TPU:9, one launch (start us, length us, event | category | flops | bytes accessed | tf_op | source)
XLA Modules:
  0.0 128.7 jit_solution(14680850857114862360)
XLA Ops:
  0.0 0.5 fusion
  0.5 125.5 %shard_map.46 = bf16[1,1536,512]{2,1,0:T(8,128)(2,1)} custom-call(bf16[1,1536,512]{2,1,0:T(8,128)(2,1)} %waves.1, bf16[1,4,1536,3072]{3,2,1,0:T(8,128)(2,1)} %operators.1, bf16[1536,512]{1,0:T(8,128)(2,1)} %sources.1, s32[1,128]{1,0:T(1,128)} %bitcast.1), custom_call_target="tpu_custom_call" | custom-call | tf_op jit(solution)/shard_map/pallas_call | solution.py:246
  126.0 2.7 %broadcast_select_fusion = bf16[1,1536,512]{2,1,0:T(8,128)(2,1)} fusion(bf16[1,1536,512]{2,1,0:T(8,128)(2,1)} %shard_map.46, pred[512]{0:T(512)(128)(4,1)} %fusion), kind=kLoop, calls=%fused_computation | loop fusion | flops 786432 | bytes 3146240 | tf_op jit(solution)/shard_map/jit(_where)/select_n | solution.py:275

commit v3 on v2

--- a/solution.py
+++ b/solution.py
@@ -9,6 +9,7 @@
 from jax.sharding import PartitionSpec as P
 
 TICKS = 3
+RELAY = 4
 MESH = pl.DeviceIdType.MESH
 
 
@@ -25,7 +26,7 @@
     layers, row_parts, chunk, big,
     waves, operators, sources, source_layer, traces,
     held, current, turned, total, outgoing, final, source_term, stage,
-    stage_sem, load_sem, store_sem, first_send, send_sem, recv_sem, final_sem,
+    stage_sem, load_sem, store_sem, row_send, send_sem, recv_sem, final_sem,
 ):
     layer = lax.axis_index("layer")
     part = lax.axis_index("row")
@@ -51,8 +52,7 @@
     for present, other in ((has_above, layer - 1), (has_below, layer + 1)):
         @pl.when(present)
         def _():
-            for p in range(row_parts):
-                pl.semaphore_signal(barrier, inc=1, device_id=(other, p), device_id_type=MESH)
+            pl.semaphore_signal(barrier, inc=1, device_id=(other, part), device_id_type=MESH)
 
     wave_load.wait()
     for i in range(rows // big):
@@ -67,27 +67,32 @@
 
     own_base = part * rows
 
+    peers = row_parts - 1 + has_above.astype(jnp.int32) + has_below.astype(jnp.int32)
+    pl.semaphore_wait(barrier, peers)
+
+    def forward(tick, group, way, span):
+        for d in range(1, row_parts):
+            pltpu.make_async_remote_copy(
+                src_ref=current.at[tick, group, way, span, :],
+                dst_ref=current.at[tick, group, way, span, :],
+                send_sem=row_send.at[tick, group, way, d - 1],
+                recv_sem=recv_sem.at[tick, group, way, part],
+                device_id=(layer, lax.rem(part + d, row_parts)),
+                device_id_type=MESH,
+            ).start()
+
     @pl.loop(0, chunks)
     def _(i):
+        span = piece(i, chunk, own_base)
         for way, groups in packed(piece(i)):
             for group in range(2):
-                current[0, group, way, piece(i, chunk, own_base), :] = groups[group].astype(jnp.bfloat16)
-
-    peers = row_parts - 1 + row_parts * (has_above.astype(jnp.int32) + has_below.astype(jnp.int32))
-    pl.semaphore_wait(barrier, peers)
+                current[0, group, way, span, :] = groups[group].astype(jnp.bfloat16)
+        forward(0, 0, 0, span)
+        forward(0, 0, 1, span)
 
     own = piece(0, rows, own_base)
-    for group in range(2):
-        for way in range(2):
-            for d in range(1, row_parts):
-                pltpu.make_async_remote_copy(
-                    src_ref=current.at[0, group, way, own, :],
-                    dst_ref=current.at[0, group, way, own, :],
-                    send_sem=first_send.at[group, way, d - 1],
-                    recv_sem=recv_sem.at[0, group, way, part],
-                    device_id=(layer, lax.rem(part + d, row_parts)),
-                    device_id_type=MESH,
-                ).start()
+    forward(0, 1, 0, own)
+    forward(0, 1, 1, own)
 
     source_load.start()
     source_load.wait()
@@ -124,22 +129,33 @@
         out += jnp.dot(held[3, span, inner], jnp.concatenate([up_turned, down_turned], 1), preferred_element_type=jnp.float32)
         return out
 
+    def take_next(step):
+        tick, group = step // 2, step % 2
+        for way, present in ((0, has_above), (1, has_below)):
+            @pl.when(jnp.logical_and(present, jnp.logical_and(step >= 2, step < 2 * TICKS)))
+            def _():
+                arrived(tick, group, way, part)
+                forward(tick, group, way, own)
+
     @pl.loop(0, 2 * TICKS)
     def _(step):
         tick, group = step // 2, step % 2
         for d in range(row_parts):
             p = lax.rem(part + d, row_parts)
             inner = pl.ds(pl.multiple_of(p * rows, 128), rows)
+            if d == min(1, row_parts - 1):
+                take_next(step + 1)
+
             if d > 0:
                 @pl.when(tick == 0)
                 def _():
                     arrived(tick, group, 0, p)
                     arrived(tick, group, 1, p)
 
-            for way, present in ((0, has_above), (1, has_below)):
-                @pl.when(jnp.logical_and(tick > 0, present))
-                def _():
-                    arrived(tick, group, way, p)
+                for way, present in ((0, has_above), (1, has_below)):
+                    @pl.when(jnp.logical_and(tick > 0, present))
+                    def _():
+                        arrived(tick, group, way, p)
 
             @pl.loop(0, chunks)
             def _(i):
@@ -180,22 +196,21 @@
                 for way, present, other in ((0, has_below, layer + 1), (1, has_above, layer - 1)):
                     @pl.when(jnp.logical_and(present, tick < TICKS - 1))
                     def _():
-                        for e in range(row_parts - 1, -1, -1):
-                            pltpu.make_async_remote_copy(
-                                src_ref=outgoing.at[tick, group, way, span, :],
-                                dst_ref=current.at[tick + 1, group, way, there, :],
-                                send_sem=send_sem.at[tick, group, way, e],
-                                recv_sem=recv_sem.at[tick + 1, group, way, part],
-                                device_id=(other, lax.rem(part + e, row_parts)),
-                                device_id_type=MESH,
-                            ).start()
+                        pltpu.make_async_remote_copy(
+                            src_ref=outgoing.at[tick, group, way, span, :],
+                            dst_ref=current.at[tick + 1, group, way, there, :],
+                            send_sem=send_sem.at[tick, group, way],
+                            recv_sem=recv_sem.at[tick + 1, group, way, part],
+                            device_id=(other, part),
+                            device_id_type=MESH,
+                        ).start()
 
                     @pl.when(jnp.logical_and(present, tick == TICKS - 1))
                     def _():
                         pltpu.make_async_remote_copy(
                             src_ref=outgoing.at[tick, group, way, span, :],
                             dst_ref=final.at[group, way, span, :],
-                            send_sem=send_sem.at[tick, group, way, 0],
+                            send_sem=send_sem.at[tick, group, way],
                             recv_sem=final_sem.at[group, way, i],
                             device_id=(other, part),
                             device_id_type=MESH,
@@ -220,21 +235,42 @@
                 stage[span, at:at + lanes] = block.astype(jnp.bfloat16)
         store(i).start()
 
+    def sent(tick, group, way):
+        for d in range(1, row_parts):
+            ref = current.at[tick, group, way, own, :]
+            pltpu.make_async_copy(ref, ref, row_send.at[tick, group, way, d - 1]).wait()
+
     for group in range(2):
-        for way, present in ((0, has_below), (1, has_above)):
-            for d in range(1, row_parts):
-                ref = current.at[0, group, way, own, :]
-                pltpu.make_async_copy(ref, ref, first_send.at[group, way, d - 1]).wait()
-
-            @pl.when(present)
+        for way, came, goes in ((0, has_above, has_below), (1, has_below, has_above)):
+            sent(0, group, way)
+
+            @pl.when(came)
+            def _():
+                for tick in range(1, TICKS):
+                    sent(tick, group, way)
+
+            @pl.when(goes)
             def _():
                 for tick in range(TICKS):
-                    for d in range(row_parts if tick < TICKS - 1 else 1):
-                        ref = outgoing.at[tick, group, way]
-                        pltpu.make_async_copy(ref, ref, send_sem.at[tick, group, way, d]).wait()
+                    ref = outgoing.at[tick, group, way]
+                    pltpu.make_async_copy(ref, ref, send_sem.at[tick, group, way]).wait()
 
     for i in range(chunks):
         store(i).wait()
+
+
+def relay(traces, result, buffer, in_sem, out_sem):
+    size = traces.shape[1] // RELAY
+    spans = [pl.ds(i * size, size) for i in range(RELAY)]
+    takes = [pltpu.make_async_copy(traces.at[:, s], buffer.at[:, s], in_sem.at[i]) for i, s in enumerate(spans)]
+    puts = [pltpu.make_async_copy(buffer.at[:, s], result.at[:, s], out_sem.at[i]) for i, s in enumerate(spans)]
+    for take in takes:
+        take.start()
+    for take, put in zip(takes, puts):
+        take.wait()
+        put.start()
+    for put in puts:
+        put.wait()
 
 
 def per_device(waves, operators, sources, source_layer):
@@ -260,8 +296,8 @@
             pltpu.SemaphoreType.DMA((2,)),
             pltpu.SemaphoreType.DMA((rows // big,)),
             pltpu.SemaphoreType.DMA((rows // chunk,)),
-            pltpu.SemaphoreType.DMA((2, 2, max(row_parts - 1, 1))),
-            pltpu.SemaphoreType.DMA((TICKS, 2, 2, row_parts)),
+            pltpu.SemaphoreType.DMA((TICKS, 2, 2, max(row_parts - 1, 1))),
+            pltpu.SemaphoreType.DMA((TICKS, 2, 2)),
             pltpu.SemaphoreType.DMA((TICKS, 2, 2, row_parts)),
             pltpu.SemaphoreType.DMA((2, 2, rows // chunk)),
         ],
@@ -269,10 +305,17 @@
             collective_id=0, has_side_effects=True, vmem_limit_bytes=67043328
         ),
     )(waves, operators, sources, source_layer.reshape(1, lanes))
-    layer = lax.axis_index("layer")
-    upgoing = lax.broadcasted_iota(jnp.int32, waves.shape, 2) >= 2 * lanes
-    edge = jnp.where(upgoing, layer == layers - 1, layer == 0)
-    return jnp.where(edge, jnp.zeros_like(traces), traces)
+    return pl.pallas_call(
+        relay,
+        out_shape=jax.ShapeDtypeStruct(traces.shape, traces.dtype),
+        in_specs=[anywhere],
+        out_specs=anywhere,
+        scratch_shapes=[
+            pltpu.VMEM(traces.shape, traces.dtype),
+            pltpu.SemaphoreType.DMA((RELAY,)),
+            pltpu.SemaphoreType.DMA((RELAY,)),
+        ],
+    )(traces)
 
 
 def solution(mesh):

time: 129 us -> 122 us (0.946)
  other arithmetic: 3.2 us -> 0 us
  Pallas kernels: 125 us -> 122 us
    pallas_call x1, Pallas kernels: 125 us -> 120 us  [per_device(): pl.pallas_call(functools.partial(kernel, layers, row_parts, chunk, big),...]
    select_n x2 -> x0, other arithmetic: 3.2 us -> none  [the longest x1 2.66 us: per_device(): return jnp.where(edge, jnp.zeros_like(traces), traces)]
    pallas_call x0 -> x1, Pallas kernels: none -> 2.2 us  [per_device(): pl.pallas_call(relay, out_shape=jax.ShapeDtypeStruct(traces.shape, traces...]
where the time goes in v3:
time: 122 us
  Pallas kernels  122 us (100%)
    pallas_call x1, Pallas kernels, per_device(): pl.pallas_call(functools.partial(kernel, layers, row_parts, chunk, big),...  120 us

profile of v3, /device:TPU:9, one launch (start us, length us, event | category | flops | bytes accessed | tf_op | source)
XLA Modules:
  0.0 122.0 jit_solution(9431029383019701466)
XLA Ops:
  0.0 119.8 %shard_map.46.traces = bf16[1,1536,512]{2,1,0:T(8,128)(2,1)} custom-call(bf16[1,1536,512]{2,1,0:T(8,128)(2,1)} %waves.1, bf16[1,4,1536,3072]{3,2,1,0:T(8,128)(2,1)} %operators.1, bf16[1536,512]{1,0:T(8,128)(2,1)} %sources.1, s32[1,128]{1,0:T(1,128)} %bitcast.1), custom_call_target="tpu_custom_call" | custom-call | tf_op jit(solution)/shard_map/pallas_call | solution.py:282
  119.8 2.2 %shard_map.47 = bf16[1,1536,512]{2,1,0:T(8,128)(2,1)} custom-call(bf16[1,1536,512]{2,1,0:T(8,128)(2,1)} %shard_map.46.traces), custom_call_target="tpu_custom_call" | custom-call | tf_op jit(solution)/shard_map/pallas_call | solution.py:308
